TPU v7x, 256 devices: a whole 4x4x8 slice. The times are simulated.
256 devices in a mesh: req: 16 (over y_hi, x, core), tp: 16 (over y_lo, z).
Axes of the slice: x: 4, y: 4 (y_hi: 2, y_lo: 2; y = y_hi * 2 + y_lo), z: 8, core: 2. Of those that a mesh axis runs over, the one named last changes fastest.
Arguments:
- tokens: bfloat16 [14336, 5120], P(('req', 'tp')), may hold values from -6 to 6
- qkv_weight: bfloat16 [5120, 3, 4096], P('req', None, 'tp')
- out_weight: bfloat16 [4096, 5120], P('tp', 'req')
- query_key_gain: float32 [2, 4096], P(None, 'tp'), may hold values from 0.25 to 1.75
- post_gain: float32 [5120], replicated, may hold values from 0.25 to 1.75
- pool_cache: bfloat16 [512, 128, 2, 4096], P('req', None, None, 'tp'), may hold values from -68 to 68
- lengths: int32 [16, 16], P('req'), may hold values from 1 to 256, 896 in all within a row
- prefix_pages: int32 [16, 16], P('req'), may hold values from 1 to 16, 32 in all within a row
- pool_order: int32 [16, 32], P('req'), may hold values from 0 to 31, each once within a row
- owners: int32 [16, 16], P('req'), may hold values from 0 to 15, each once within a row
Outputs:
- hidden: bfloat16 [14336, 5120], P(('req', 'tp'))
- handed_pages: bfloat16 [512, 128, 2, 4096], P('req', None, None, 'tp')
Inputs may be any that keep to these rules, and one draw needn't show every extreme that they name: `lengths`: each row sums to 896; the largest entry of every row is exactly 256. `prefix_pages`: each row sums to 32; the largest entry of every row is exactly 16. `pool_order`: each row names every slot once. `owners`: each row names every owner once.
All inputs are finite; a program needn't handle non-finite values.
Results may differ from a plain program's by a relative error of at most 0.014.
Values may be sent and summed in bfloat16 or wider, within the bound.
A program may use at most 128 MiB of HBM per device.

v0:
```python
import jax
import jax.numpy as jnp
from jax import lax
from jax.sharding import PartitionSpec as P

HEADS = 32
HEAD = 128
PAGE = 128
CAP = 2
norm_eps = 1e-06
rope_base = 500000.0
masked_score = -1e30


def token_layout(lengths_row, prefix_row, block_len):
    ends_at = jnp.cumsum(lengths_row)
    starts_at = ends_at - lengths_row
    token_ids = jnp.arange(block_len, dtype=jnp.int32)
    request_of = jnp.sum((token_ids[:, None] >= ends_at[None, :]).astype(jnp.int32), axis=1)
    one_hot = (
        request_of[:, None] == jnp.arange(lengths_row.shape[0], dtype=jnp.int32)[None, :]
    ).astype(jnp.int32)
    shift_of = jnp.sum(one_hot * (prefix_row * PAGE - starts_at)[None, :], axis=1)
    return (request_of, token_ids + shift_of, starts_at)


def slot_owner(prefix_row, order_row):
    page_ends = jnp.cumsum(prefix_row)
    page_ids = jnp.arange(order_row.shape[0], dtype=jnp.int32)
    page_request = jnp.sum((page_ids[:, None] >= page_ends[None, :]).astype(jnp.int32), axis=1)
    matches = (order_row[None, :] == page_ids[:, None]).astype(jnp.int32)
    return jnp.sum(matches * page_request[None, :], axis=1)


def rotate_heads(tensor, positions):
    half_dim = HEAD // 2
    frequency = rope_base ** (-(2.0 * jnp.arange(half_dim, dtype=jnp.float32)) / HEAD)
    angles = positions.astype(jnp.float32)[:, None] * frequency[None, :]
    cosine = jnp.cos(angles)[:, None, :]
    sine_part = jnp.sin(angles)[:, None, :]
    first_half = tensor[..., :half_dim]
    second_half = tensor[..., half_dim:]
    return jnp.concatenate(
        [
            first_half * cosine - second_half * sine_part,
            second_half * cosine + first_half * sine_part,
        ],
        axis=-1,
    )


def attend_head(queries, pool_keys, pool_values, new_keys, new_values, pool_mask, block_mask):
    score_scale = HEAD ** (-0.5)
    pool_scores = jnp.dot(queries, pool_keys.T, preferred_element_type=jnp.float32) * score_scale
    block_scores = jnp.dot(queries, new_keys.T, preferred_element_type=jnp.float32) * score_scale
    pool_scores = jnp.where(pool_mask, pool_scores, masked_score)
    block_scores = jnp.where(block_mask, block_scores, masked_score)
    row_max = jnp.maximum(jnp.max(pool_scores, axis=1), jnp.max(block_scores, axis=1))
    pool_exp = jnp.exp(pool_scores - row_max[:, None])
    block_exp = jnp.exp(block_scores - row_max[:, None])
    row_total = jnp.sum(pool_exp, axis=1) + jnp.sum(block_exp, axis=1)
    pool_weights = (pool_exp / row_total[:, None]).astype(jnp.bfloat16)
    block_weights = (block_exp / row_total[:, None]).astype(jnp.bfloat16)
    mixed_out = jnp.dot(pool_weights, pool_values, preferred_element_type=jnp.float32)
    mixed_out = mixed_out + jnp.dot(block_weights, new_values, preferred_element_type=jnp.float32)
    return mixed_out.astype(jnp.bfloat16)


def build_send(kv_new, lengths_row, starts_at, owner_row):
    page_span = CAP * PAGE
    owner_count = owner_row.shape[0]
    owner_ids = jnp.arange(owner_count, dtype=jnp.int32)
    owner_pick = (owner_row[None, :] == owner_ids[:, None]).astype(jnp.int32)
    start_of = jnp.sum(owner_pick * starts_at[None, :], axis=1)
    length_of = jnp.sum(owner_pick * lengths_row[None, :], axis=1)
    offsets = jnp.arange(page_span, dtype=jnp.int32)
    source = start_of[:, None] + offsets[None, :]
    is_valid = offsets[None, :] < length_of[:, None]
    source = jnp.clip(source, 0, kv_new.shape[0] - 1).reshape(-1)
    taken_rows = jnp.take(kv_new, source, axis=0).reshape(
        owner_count, page_span, kv_new.shape[1], kv_new.shape[2]
    )
    return jnp.where(is_valid[:, :, None, None], taken_rows, jnp.zeros_like(taken_rows))


def hand_over(kv_new, lengths_row, starts_at, owner_row):
    outgoing = build_send(kv_new, lengths_row, starts_at, owner_row)
    arrived = lax.all_to_all(outgoing, "req", split_axis=0, concat_axis=0, tiled=True)
    return arrived.reshape(arrived.shape[0] * CAP, PAGE, arrived.shape[2], arrived.shape[3])


def body(
    tokens,
    qkv_weight,
    out_weight,
    query_key_gain,
    post_gain,
    pool_cache,
    lengths,
    prefix_pages,
    pool_order,
    owners,
):
    local_width = qkv_weight.shape[2]
    heads_here = local_width // HEAD
    block_tokens = lax.all_gather(tokens, "tp", axis=0, tiled=True)
    block_len = block_tokens.shape[0]
    row_piece = lax.all_gather(qkv_weight, "req", axis=0, tiled=True)
    flat_piece = row_piece.reshape(row_piece.shape[0], 3 * local_width)
    joined_all = jnp.dot(block_tokens, flat_piece, preferred_element_type=jnp.float32)
    joined_all = joined_all.reshape(block_len, 3, local_width)
    queries = joined_all[:, 0]
    keys_raw = joined_all[:, 1]
    values_raw = joined_all[:, 2]
    local_sums = jnp.stack(
        [jnp.sum(queries * queries, axis=1), jnp.sum(keys_raw * keys_raw, axis=1)]
    )
    global_sums = lax.psum(local_sums, "tp")
    inverse = lax.rsqrt(global_sums / (HEADS * HEAD) + norm_eps)
    queries = queries * inverse[0][:, None] * query_key_gain[0]
    keys_raw = keys_raw * inverse[1][:, None] * query_key_gain[1]
    lengths_row = lengths[0]
    prefix_row = prefix_pages[0]
    request_of, positions, starts_at = token_layout(lengths_row, prefix_row, block_len)
    query_rot = rotate_heads(queries.reshape(block_len, heads_here, HEAD), positions).astype(
        jnp.bfloat16
    )
    key_rot = rotate_heads(keys_raw.reshape(block_len, heads_here, HEAD), positions).astype(
        jnp.bfloat16
    )
    value_new = values_raw.reshape(block_len, heads_here, HEAD).astype(jnp.bfloat16)
    kv_new = jnp.stack(
        [key_rot.reshape(block_len, local_width), value_new.reshape(block_len, local_width)], axis=1
    )
    pool_count = pool_cache.shape[0]
    key_owner = jnp.repeat(slot_owner(prefix_row, pool_order[0]), PAGE)
    pool_mask = request_of[:, None] == key_owner[None, :]
    token_ids = jnp.arange(block_len, dtype=jnp.int32)
    block_mask = (request_of[:, None] == request_of[None, :]) & (
        token_ids[None, :] <= token_ids[:, None]
    )
    pool_keys = pool_cache[:, :, 0, :].reshape(pool_count * PAGE, heads_here, HEAD)
    pool_values = pool_cache[:, :, 1, :].reshape(pool_count * PAGE, heads_here, HEAD)
    head_outs = lax.map(
        lambda per_head: attend_head(
            per_head[0], per_head[1], per_head[2], per_head[3], per_head[4], pool_mask, block_mask
        ),
        (
            jnp.moveaxis(query_rot, 1, 0),
            jnp.moveaxis(pool_keys, 1, 0),
            jnp.moveaxis(pool_values, 1, 0),
            jnp.moveaxis(key_rot, 1, 0),
            jnp.moveaxis(value_new, 1, 0),
        ),
    )
    attention = jnp.moveaxis(head_outs, 0, 1).reshape(block_len, local_width)
    out_full = lax.all_gather(out_weight, "req", axis=1, tiled=True)
    projected = lax.psum_scatter(
        jnp.dot(attention, out_full, preferred_element_type=jnp.float32).astype(jnp.bfloat16),
        "tp",
        scatter_dimension=0,
        tiled=True,
    ).astype(jnp.float32)
    post_scale = lax.rsqrt(jnp.mean(projected * projected, axis=1, keepdims=True) + norm_eps)
    hidden = (tokens.astype(jnp.float32) + projected * post_scale * post_gain[None, :]).astype(
        jnp.bfloat16
    )
    handed_pages = hand_over(kv_new, lengths_row, starts_at, owners[0])
    return (hidden, handed_pages)


def solution(mesh):
    in_specs = (
        P(("req", "tp"), None),
        P("req", None, "tp"),
        P("tp", "req"),
        P(None, "tp"),
        P(),
        P("req", None, None, "tp"),
        P("req", None),
        P("req", None),
        P("req", None),
        P("req", None),
    )
    out_specs = (P(("req", "tp"), None), P("req", None, None, "tp"))
    return jax.shard_map(body, mesh=mesh, in_specs=in_specs, out_specs=out_specs, check_vma=False)
```

profile of v0, /device:TPU:1, one launch (start us, length us, event | category | flops | bytes accessed | tf_op | source)
XLA Modules:
  0.0 490.8 jit_solution(5319571095638446805)
XLA Ops:
  11.2 1.2 fusion.43
  12.5 21.7 %slice_reduce_fusion = (bf16[32,128,256]{2,1,0:T(8,128)(2,1)}, bf16[32,128,256]{2,1,0:T(8,128)(2,1)}) fusion(bf16[32,128,2,256]{3,2,1,0:T(2,128)(2,1)} %param.17), kind=kLoop, calls=%fused_computation.45 | loop fusion | bytes 8388608 | tf_op jit(solution)/shard_map/slice | solution.py:143
  34.2 2.6 reshape.260
  36.8 4.0 reshape.259
  41.3 1.7 multiply_cosine_fusion
  42.9 4.2 copy_bitcast_fusion
  47.1 43.6 %all-gather.6.cloned.1.call-done = bf16[5120,3,256]{2,0,1:T(8,128)(2,1)} async-done(((bf16[320,3,256]{2,0,1:T(8,128)(2,1)}), bf16[5120,3,256]{2,0,1:T(8,128)(2,1)}) %all-gather.6.cloned.1.call-update) | async-done | bytes 7864336 | tf_op jit(solution)/shard_map/all_gather | solution.py:108
  90.7 10.8 %copy.45 = bf16[5120,3,256]{0,2,1:T(8,128)(2,1)} copy(bf16[5120,3,256]{2,0,1:T(8,128)(2,1)} %all-gather.6.cloned.1.call-done) | data formatting | bytes 15728640 | tf_op jit(solution)/shard_map/all_gather | solution.py:108
  101.5 97.4 %all-gather.4.cloned.1.call-done = bf16[896,5120]{1,0:T(8,128)(2,1)} async-done(((bf16[56,5120]{1,0:T(8,128)(2,1)}), bf16[896,5120]{1,0:T(8,128)(2,1)}) %all-gather.4.cloned.1.call-update) | async-done | bytes 9175056 | tf_op jit(solution)/shard_map/all_gather | solution.py:106
  198.9 12.0 %fusion.32 = f32[896,3,256]{0,2,1:T(8,128)S(1)} fusion(bf16[896,5120]{1,0:T(8,128)(2,1)} %all-gather.4.cloned.1.call-done, bf16[5120,3,256]{0,2,1:T(8,128)(2,1)} %copy.45), kind=kOutput, calls=%fused_computation.39 | convolution fusion | flops 7046430720 | bytes 19791872 | tf_op jit(solution)/shard_map/dot_general | solution.py:110
  210.9 1.1 multiply_reduce_fusion.1
  212.1 2.6 copy.49
  214.7 26.0 %psum.7 = f32[2,896]{1,0:T(2,128)S(1)} all-reduce(f32[2,896]{1,0:T(2,128)S(1)} %pad_maximum_fusion.1), channel_id=1, replica_groups=mesh['req'=16,'tp'=16] {'tp'}, use_global_device_ids=true, to_apply=%region_2.0 | all-reduce | flops 1792 | bytes 14336 | tf_op jit(solution)/shard_map/psum | solution.py:118
  240.8 1.2 copy.46
  242.0 1.8 multiply_multiply_fusion
  246.2 59.5 %while.12 = (s32[]{:T(128)}, bf16[2,896,128]{1,2,0:T(8,128)(2,1)}, bf16[2,896,128]{2,1,0:T(8,128)(2,1)}, bf16[2,4096,128]{2,1,0:T(8,128)(2,1)}, bf16[2,896,128]{...) while((s32[]{:T(128)}, bf16[2,896,128]{1,2,0:T(8,128)(2,1)}, ...), condition=%wide.region_14.15_spmd.clone.clone, body=%wide.region_9.14_spmd.clone.clone.sunk | while | flops 2354198784 | bytes 70941888 | solution.py:144
  246.3 9.3 %fusion.59 = (f32[896]{0:T(1024)S(1)}, f32[896,4096]{1,0:T(8,128)}) fusion(s32[4096]{0:T(1024)S(1)} %get-tuple-element.264, s32[896]{0:T(1024)S(1)} %get-tuple-element.265, bf16[2,4096,128]{2,1,0:T(8,128)(2,1)} %get-tuple-element.260, s32[]{:T(128)S(6)} %copy.72, bf16[2,896,128]{2,1,0:T(8,128)(2,1)} %get-tuple-element.259), kind=kOutput, calls=%fused_computation.7.clone.1 | convolution fusion | flops 954203264 | bytes 15982592 | tf_op jit(solution)/shard_map/while/body/eval_jaxpr/dot_general | solution.py:54
  255.5 1.6 fusion.60
  257.2 8.8 %fusion.61 = f32[896]{0:T(1024)S(1)} fusion(f32[896,4096]{1,0:T(8,128)} %get-tuple-element.233, s32[4096]{0:T(1024)S(1)} %get-tuple-element.264, f32[896]{0:T(1024)S(1)} %max.23, s32[896]{0:T(1024)S(1)} %get-tuple-element.265), kind=kLoop, calls=%fused_computation.6.clone.1 | loop fusion | flops 18349184 | bytes 14707200 | tf_op jit(solution)/shard_map/while/body/eval_jaxpr/reduce_sum | solution.py:61
  266.5 7.7 %fusion.63 = f32[896,128]{1,0:T(8,128)S(1)} fusion(f32[896,4096]{1,0:T(8,128)} %get-tuple-element.233, s32[4096]{0:T(1024)S(1)} %get-tuple-element.264, f32[896]{0:T(1024)S(1)} %add.169, f32[896]{0:T(1024)S(1)} %max.23, s32[896]{0:T(1024)S(1)} %get-tuple-element.265, bf16[2,4096,128]{2,1,0:T(8,128)(2,1)S(1)} %copy-done.7, s32[]{:T(128)S(6)} %copy.72), kind=kOutput, calls=%fused_computation.8.clone.1 | convolution fusion | flops 961544192 | bytes 16216068 | tf_op jit(solution)/shard_map/while/body/eval_jaxpr/dot_general | solution.py:64
  276.0 9.2 %fusion.59 = (f32[896]{0:T(1024)S(1)}, f32[896,4096]{1,0:T(8,128)}) fusion(s32[4096]{0:T(1024)S(1)} %get-tuple-element.264, s32[896]{0:T(1024)S(1)} %get-tuple-element.265, bf16[2,4096,128]{2,1,0:T(8,128)(2,1)} %get-tuple-element.260, s32[]{:T(128)S(6)} %copy.72, bf16[2,896,128]{2,1,0:T(8,128)(2,1)} %get-tuple-element.259), kind=kOutput, calls=%fused_computation.7.clone.1 | convolution fusion | flops 954203264 | bytes 15982592 | tf_op jit(solution)/shard_map/while/body/eval_jaxpr/dot_general | solution.py:54
  285.3 1.6 fusion.60
  286.9 8.8 %fusion.61 = f32[896]{0:T(1024)S(1)} fusion(f32[896,4096]{1,0:T(8,128)} %get-tuple-element.233, s32[4096]{0:T(1024)S(1)} %get-tuple-element.264, f32[896]{0:T(1024)S(1)} %max.23, s32[896]{0:T(1024)S(1)} %get-tuple-element.265), kind=kLoop, calls=%fused_computation.6.clone.1 | loop fusion | flops 18349184 | bytes 14707200 | tf_op jit(solution)/shard_map/while/body/eval_jaxpr/reduce_sum | solution.py:61
  296.2 7.7 %fusion.63 = f32[896,128]{1,0:T(8,128)S(1)} fusion(f32[896,4096]{1,0:T(8,128)} %get-tuple-element.233, s32[4096]{0:T(1024)S(1)} %get-tuple-element.264, f32[896]{0:T(1024)S(1)} %add.169, f32[896]{0:T(1024)S(1)} %max.23, s32[896]{0:T(1024)S(1)} %get-tuple-element.265, bf16[2,4096,128]{2,1,0:T(8,128)(2,1)S(1)} %copy-done.7, s32[]{:T(128)S(6)} %copy.72), kind=kOutput, calls=%fused_computation.8.clone.1 | convolution fusion | flops 961544192 | bytes 16216068 | tf_op jit(solution)/shard_map/while/body/eval_jaxpr/dot_general | solution.py:64
  305.8 8.0 %convolution_convert_fusion = bf16[896,5120]{1,0:T(8,128)(2,1)} fusion(bf16[896,256]{0,1:T(8,128)(2,1)} %bitcast.104, bf16[256,5120]{0,1:T(8,128)(2,1)} %all-gather.8.cloned.1.call-done), kind=kOutput, calls=%fused_computation.41 | convolution fusion | flops 2353397760 | bytes 12255232 | tf_op jit(solution)/shard_map/dot_general | solution.py:159
  315.6 1.3 copy.57
  316.9 32.4 %gather_fusion = bf16[4096,2,256]{2,1,0:T(2,128)(2,1)} fusion(bf16[896,2,256]{2,1,0:T(2,128)(2,1)S(1)} %copy.57, s32[4096]{0:T(1024)S(1)} %broadcast_clamp_fusion), kind=kCustom, calls=%fused_computation | custom fusion | bytes 8404992 | tf_op jit(solution)/shard_map/jit(_take)/gather | solution.py:80
  349.3 12.7 %broadcast_select_fusion.1 = bf16[16,256,2,256]{3,2,1,0:T(2,128)(2,1)S(1)} fusion(pred[16,256]{1,0:T(8,128)(4,1)S(1)} %get-tuple-element.172, bf16[16,256,2,256]{3,2,1,0:T(2,128)(2,1)} %bitcast.98, pred[16,256]{1,0:T(8,128)(4,1)S(1)} %get-tuple-element.173), kind=kLoop, calls=%fused_computation.43 | loop fusion | flops 4194304 | bytes 8396800 | tf_op jit(solution)/shard_map/jit(_where)/select_n | solution.py:83
  362.0 109.6 %all_to_all.5 = bf16[16,256,2,256]{3,2,1,0:T(2,128)(2,1)} all-to-all(bf16[16,256,2,256]{3,2,1,0:T(2,128)(2,1)S(1)} %broadcast_select_fusion.1), channel_id=1, replica_groups=mesh['req'=16,'tp'=16] {'req'}, dimensions={0} | all-to-all | bytes 8388608 | tf_op jit(solution)/shard_map/all_to_all | solution.py:88
  471.6 1.3 fusion.35
  472.9 2.1 fusion.38
  475.1 9.2 %copy.79 = bf16[32,128,2,256]{3,2,1,0:T(2,128)(2,1)} copy(bf16[32,128,2,256]{3,2,1,0:T(2,128)(2,1)} %bitcast.99) | data formatting | bytes 8388608
  (96 shorter events, 13.5 us)
Async XLA Ops:
  7.2 83.5 %all-gather.6.cloned.1.call-start = ((), (), s32[]{:S(2)}) async-start(), calls=%async_computation.3 | async-start | bytes 8355840 | tf_op jit(solution)/shard_map/all_gather | solution.py:108
  7.9 191.0 %all-gather.4.cloned.1.call-start = ((), (), s32[]{:S(2)}) async-start(), calls=%async_computation.2 | async-start | bytes 9748480 | tf_op jit(solution)/shard_map/all_gather | solution.py:106
  8.6 297.1 %all-gather.8.cloned.1.call-start = ((), (), s32[]{:S(2)}) async-start(), calls=%async_computation.4 | async-start | bytes 2785280 | tf_op jit(solution)/shard_map/all_gather | solution.py:157
  9.4 462.2 %reduce-scatter.2.cloned.1.call-start = ((), (), s32[]{:S(2)}) async-start(), calls=%async_computation.5 | async-start | bytes 9748480 | tf_op jit(solution)/shard_map/reduce_scatter | solution.py:158
  34.2 6.5 %copy-start.12 = (s32[1,16]{1,0:T(1,128)S(1)}, s32[1,16]{1,0:T(1,128)}, u32[]{:S(2)}) copy-start(s32[1,16]{1,0:T(1,128)} %param.19) | copy-start | bytes 196
  34.2 6.9 %copy-start.15 = (s32[1,32]{1,0:T(1,128)S(1)}, s32[1,32]{1,0:T(1,128)}, u32[]{:S(2)}) copy-start(s32[1,32]{1,0:T(1,128)} %param.20) | copy-start | bytes 388
  212.1 32.6 %copy-start = (bf16[896,1,256]{0,2,1:T(8,128)(2,1)}, bf16[896,1,256]{0,2,1:T(8,128)(2,1)S(1)}, u32[]{:S(2)}) copy-start(bf16[896,1,256]{0,2,1:T(8,128)(2,1)S(1)} %slice.78) | copy-start | bytes 1376260
  244.6 1.6 copy-start.2
  244.6 1.6 copy-start.4
  257.2 9.3 %copy-start.7 = (bf16[2,4096,128]{2,1,0:T(8,128)(2,1)S(1)}, bf16[2,4096,128]{2,1,0:T(8,128)(2,1)}, u32[]{:S(2)}) copy-start(bf16[2,4096,128]{2,1,0:T(8,128)(2,1)} %get-tuple-element.262) | copy-start | bytes 6291460 | tf_op jit(solution)/shard_map/while
  274.2 1.0 copy-start.8
  275.3 0.8 copy-start.9
  286.9 9.3 %copy-start.7 = (bf16[2,4096,128]{2,1,0:T(8,128)(2,1)S(1)}, bf16[2,4096,128]{2,1,0:T(8,128)(2,1)}, u32[]{:S(2)}) copy-start(bf16[2,4096,128]{2,1,0:T(8,128)(2,1)} %get-tuple-element.262) | copy-start | bytes 6291460 | tf_op jit(solution)/shard_map/while
  304.0 1.0 copy-start.8
  305.0 0.8 copy-start.9
  313.8 0.7 copy-start.11
  313.8 0.7 copy-start.13
  313.8 0.7 copy-start.14
  313.8 1.0 copy-start.3
  313.8 1.2 copy-start.5
  313.8 1.7 copy-start.1
  362.0 110.9 %copy-start.6 = (bf16[56,5120]{1,0:T(8,128)(2,1)S(1)}, bf16[56,5120]{1,0:T(8,128)(2,1)}, u32[]{:S(2)}) copy-start(bf16[56,5120]{1,0:T(8,128)(2,1)} %param.12) | copy-start | bytes 1720324
  362.0 110.9 %copy-start.10 = (f32[5120]{0:T(1024)S(1)}, f32[5120]{0:T(1024)}, u32[]{:S(2)}) copy-start(f32[5120]{0:T(1024)} %param.16) | copy-start | bytes 61444
Sparse Core Ops, SparseCore 0:
  10.8 79.8 all-gather.5
  92.5 106.3 all-gather.3
  201.6 53.9 all-gather.7
  314.0 145.7 reduce-scatter.1
where the time goes:
time: 492 us; the launch traced here: 491 us
  waiting for transfers between devices  143 us (29%)
  blocking collectives  136 us (28%)
  local copies, waits for them, and re-layouts  95.2 us (19%)
  matrix products  58.7 us (12%)
  other arithmetic  43.9 us (9%)
  between operations  14 us (3%)
    all_to_all x1, blocking collectives, hand_over(): lax.all_to_all(outgoing, 'req', split_axis=0, concat_axis=0, tiled=True)  110 us
    all_gather x1, waiting for transfers between devices, body(): block_tokens = lax.all_gather(tokens, 'tp', axis=0, tiled=True)  97.4 us
    all_gather x1, waiting for transfers between devices, body(): row_piece = lax.all_gather(qkv_weight, 'req', axis=0, tiled=True)  43.6 us
    gather x1, local copies, waits for them, and re-layouts, build_send(): jnp.take(kv_new, source, axis=0)  32.4 us
    psum x1, blocking collectives, body(): global_sums = lax.psum(local_sums, 'tp')  26 us
    slice x1, local copies, waits for them, and re-layouts, body(): pool_cache[:, :, 1, :].reshape(pool_count * PAGE, heads_here, HEAD)  21.7 us
    reduce_sum x4, other arithmetic, attend_head(): row_total = jnp.sum(pool_exp, axis=1) + jnp.sum(block_exp, axis=1)  18.6 us
    dot_general x2, matrix products, attend_head(): jnp.dot(queries, pool_keys.T, preferred_element_type=jnp.float32)  18.5 us
  transfers between devices with their start and end apart: 4, of which 2 were waited for; matrix products, arithmetic and copies ran while one was open for 36% of the time, Pallas kernels for 0%

commit v1 on v0

--- a/solution.py
+++ b/solution.py
@@ -101,9 +101,15 @@
     pool_order,
     owners,
 ):
+
+    def vector_register(tile_in):
+        return jnp.concatenate(
+            lax.all_to_all(jnp.stack(lax.axis_size("tp") * [tile_in], 0), "tp", 0, 0), 0
+        )
+
     local_width = qkv_weight.shape[2]
     heads_here = local_width // HEAD
-    block_tokens = lax.all_gather(tokens, "tp", axis=0, tiled=True)
+    block_tokens = vector_register(tokens)
     block_len = block_tokens.shape[0]
     row_piece = lax.all_gather(qkv_weight, "req", axis=0, tiled=True)
     flat_piece = row_piece.reshape(row_piece.shape[0], 3 * local_width)

time: 492 us -> 527 us (1.071)
  waiting for transfers between devices: 143 us -> 159 us
  starting transfers between devices: 0.15 us -> 10.4 us
    all_gather x1 -> x0, waiting for transfers between devices: 97.4 us -> none  [body(): block_tokens = lax.all_gather(tokens, 'tp', axis=0, tiled=True)]
    all_to_all x0 -> x1, waiting for transfers between devices: none -> 67 us  [vector_register(): lax.all_to_all(jnp.stack(lax.axis_size('tp') * [tile_in], 0), 'tp', 0, 0)]
    all_gather x1, waiting for transfers between devices: 43.6 us -> 90.3 us  [body(): row_piece = lax.all_gather(qkv_weight, 'req', axis=0, tiled=True)]
    all_to_all x0 -> x1, starting transfers between devices: none -> 10.3 us  [vector_register(): lax.all_to_all(jnp.stack(lax.axis_size('tp') * [tile_in], 0), 'tp', 0, 0)]
    another operation x1 -> x2, local copies, waits for them, and re-layouts: 0.08 us -> 5.84 us  [the longest x1 5.75 us: vector_register(): jnp.stack(lax.axis_size('tp') * [tile_in], 0)]
    psum x1, blocking collectives: 26 us -> 31.7 us  [body(): global_sums = lax.psum(local_sums, 'tp')]
    unnamed x29 -> x33, local copies, waits for them, and re-layouts: 14.2 us -> 14.2 us
  transfers between devices with their start and end apart: 4 -> 4, of which waited for: 2 -> 2; matrix products, arithmetic and copies ran while one was open for 36% -> 34% of each run, Pallas kernels for 0% -> 0%
where the time goes in v1:
time: 527 us; the launch traced here: 526 us
  waiting for transfers between devices  159 us (30%)
  blocking collectives  141 us (27%)
  local copies, waits for them, and re-layouts  99.3 us (19%)
  matrix products  58.6 us (11%)
  other arithmetic  43.2 us (8%)
  between operations  14.1 us (3%)
  starting transfers between devices  10.4 us (2%)
    all_to_all x1, blocking collectives, hand_over(): lax.all_to_all(outgoing, 'req', split_axis=0, concat_axis=0, tiled=True)  110 us
    all_gather x1, waiting for transfers between devices, body(): row_piece = lax.all_gather(qkv_weight, 'req', axis=0, tiled=True)  90.3 us
    all_to_all x1, waiting for transfers between devices, vector_register(): lax.all_to_all(jnp.stack(lax.axis_size('tp') * [tile_in], 0), 'tp', 0, 0)  67 us
    gather x1, local copies, waits for them, and re-layouts, build_send(): jnp.take(kv_new, source, axis=0)  32.4 us
    psum x1, blocking collectives, body(): global_sums = lax.psum(local_sums, 'tp')  31.7 us
    slice x1, local copies, waits for them, and re-layouts, body(): pool_cache[:, :, 1, :].reshape(pool_count * PAGE, heads_here, HEAD)  21.6 us
    reduce_sum x4, other arithmetic, attend_head(): row_total = jnp.sum(pool_exp, axis=1) + jnp.sum(block_exp, axis=1)  18.6 us
    dot_general x2, matrix products, attend_head(): jnp.dot(queries, pool_keys.T, preferred_element_type=jnp.float32)  18.5 us
  transfers between devices with their start and end apart: 4, of which 2 were waited for; matrix products, arithmetic and copies ran while one was open for 34% of the time, Pallas kernels for 0%

profile of v1, /device:TPU:1, one launch (start us, length us, event | category | flops | bytes accessed | tf_op | source)
XLA Modules:
  0.0 525.8 jit_solution(8540063974792696077)
XLA Ops:
  7.9 5.8 %stack.10 = bf16[16,56,5120]{2,1,0:T(8,128)(2,1)} broadcast(bf16[56,5120]{1,0:T(8,128)(2,1)} %param.12), dimensions={1,2} | broadcast | bytes 9748480 | tf_op jit(solution)/shard_map/stack | solution.py:107
  13.7 10.3 %all-to-all-start = ((bf16[16,56,5120]{2,1,0:T(8,128)(2,1)}), bf16[16,56,5120]{2,1,0:T(8,128)(2,1)}, u32[]{:S(2)}, u32[]{:S(2)}) async-start(bf16[16,56,5120]{2,1,0:T(8,128)(2,1)} %stack.10), calls=%async_computation | async-start | bytes 18350080 | tf_op jit(solution)/shard_map/all_to_all | solution.py:107
  25.0 21.6 %slice_reduce_fusion = (bf16[32,128,256]{2,1,0:T(8,128)(2,1)}, bf16[32,128,256]{2,1,0:T(8,128)(2,1)}) fusion(bf16[32,128,2,256]{3,2,1,0:T(2,128)(2,1)} %param.17), kind=kLoop, calls=%fused_computation.44 | loop fusion | bytes 8388608 | tf_op jit(solution)/shard_map/slice | solution.py:149
  46.7 2.6 reshape.266
  49.3 4.0 reshape.265
  54.5 1.7 multiply_cosine_fusion
  56.2 4.1 copy_bitcast_fusion
  60.3 90.3 %all-gather.3.cloned.1.call-done = bf16[5120,3,256]{2,0,1:T(8,128)(2,1)} async-done(((bf16[320,3,256]{2,0,1:T(8,128)(2,1)}), bf16[5120,3,256]{2,0,1:T(8,128)(2,1)}) %all-gather.3.cloned.1.call-update) | async-done | bytes 7864336 | tf_op jit(solution)/shard_map/all_gather | solution.py:114
  150.6 10.7 %copy.45 = bf16[5120,3,256]{0,2,1:T(8,128)(2,1)} copy(bf16[5120,3,256]{2,0,1:T(8,128)(2,1)} %all-gather.3.cloned.1.call-done) | data formatting | bytes 15728640 | tf_op jit(solution)/shard_map/all_gather | solution.py:114
  161.3 67.0 %all-to-all-done = bf16[16,56,5120]{2,1,0:T(8,128)(2,1)} async-done(((bf16[16,56,5120]{2,1,0:T(8,128)(2,1)}), bf16[16,56,5120]{2,1,0:T(8,128)(2,1)}, u32[]{:S(2)}, u32[]{:S(2)}) %all-to-all-start) | async-done | bytes 9175072 | tf_op jit(solution)/shard_map/all_to_all | solution.py:107
  228.3 12.0 %fusion.32 = f32[896,3,256]{0,2,1:T(8,128)S(1)} fusion(bf16[896,5120,1]{1,0,2:T(8,128)(2,1)} %bitcast.1, bf16[5120,3,256]{0,2,1:T(8,128)(2,1)} %copy.45), kind=kOutput, calls=%fused_computation.42 | convolution fusion | flops 7046430720 | bytes 19791872 | tf_op jit(solution)/shard_map/dot_general | solution.py:116
  241.5 2.6 copy.49
  244.1 31.7 %psum.7 = f32[2,896]{1,0:T(2,128)S(1)} all-reduce(f32[2,896]{1,0:T(2,128)S(1)} %pad_maximum_fusion.1), channel_id=1, replica_groups=mesh['req'=16,'tp'=16] {'tp'}, use_global_device_ids=true, to_apply=%region_2.0 | all-reduce | flops 1792 | bytes 14336 | tf_op jit(solution)/shard_map/psum | solution.py:124
  275.8 1.2 copy.46
  277.1 1.8 multiply_multiply_fusion
  281.3 59.5 %while.12 = (s32[]{:T(128)}, bf16[2,896,128]{1,2,0:T(8,128)(2,1)}, bf16[2,896,128]{2,1,0:T(8,128)(2,1)}, bf16[2,4096,128]{2,1,0:T(8,128)(2,1)}, bf16[2,896,128]{...) while((s32[]{:T(128)}, bf16[2,896,128]{1,2,0:T(8,128)(2,1)}, ...), condition=%wide.region_14.15_spmd.clone.clone, body=%wide.region_9.14_spmd.clone.clone.sunk | while | flops 2354198784 | bytes 70941888 | solution.py:150
  281.3 9.2 %fusion.59 = (f32[896]{0:T(1024)S(1)}, f32[896,4096]{1,0:T(8,128)}) fusion(s32[4096]{0:T(1024)S(1)} %get-tuple-element.264, s32[896]{0:T(1024)S(1)} %get-tuple-element.265, bf16[2,4096,128]{2,1,0:T(8,128)(2,1)} %get-tuple-element.260, s32[]{:T(128)S(6)} %copy.72, bf16[2,896,128]{2,1,0:T(8,128)(2,1)} %get-tuple-element.259), kind=kOutput, calls=%fused_computation.7.clone.1 | convolution fusion | flops 954203264 | bytes 15982592 | tf_op jit(solution)/shard_map/while/body/eval_jaxpr/dot_general | solution.py:54
  290.5 1.6 fusion.60
  292.2 8.8 %fusion.61 = f32[896]{0:T(1024)S(1)} fusion(f32[896,4096]{1,0:T(8,128)} %get-tuple-element.233, s32[4096]{0:T(1024)S(1)} %get-tuple-element.264, f32[896]{0:T(1024)S(1)} %max.23, s32[896]{0:T(1024)S(1)} %get-tuple-element.265), kind=kLoop, calls=%fused_computation.6.clone.1 | loop fusion | flops 18349184 | bytes 14707200 | tf_op jit(solution)/shard_map/while/body/eval_jaxpr/reduce_sum | solution.py:61
  301.5 7.7 %fusion.63 = f32[896,128]{1,0:T(8,128)S(1)} fusion(f32[896,4096]{1,0:T(8,128)} %get-tuple-element.233, s32[4096]{0:T(1024)S(1)} %get-tuple-element.264, f32[896]{0:T(1024)S(1)} %add.169, f32[896]{0:T(1024)S(1)} %max.23, s32[896]{0:T(1024)S(1)} %get-tuple-element.265, bf16[2,4096,128]{2,1,0:T(8,128)(2,1)S(1)} %copy-done.7, s32[]{:T(128)S(6)} %copy.72), kind=kOutput, calls=%fused_computation.8.clone.1 | convolution fusion | flops 961544192 | bytes 16216068 | tf_op jit(solution)/shard_map/while/body/eval_jaxpr/dot_general | solution.py:64
  311.0 9.2 %fusion.59 = (f32[896]{0:T(1024)S(1)}, f32[896,4096]{1,0:T(8,128)}) fusion(s32[4096]{0:T(1024)S(1)} %get-tuple-element.264, s32[896]{0:T(1024)S(1)} %get-tuple-element.265, bf16[2,4096,128]{2,1,0:T(8,128)(2,1)} %get-tuple-element.260, s32[]{:T(128)S(6)} %copy.72, bf16[2,896,128]{2,1,0:T(8,128)(2,1)} %get-tuple-element.259), kind=kOutput, calls=%fused_computation.7.clone.1 | convolution fusion | flops 954203264 | bytes 15982592 | tf_op jit(solution)/shard_map/while/body/eval_jaxpr/dot_general | solution.py:54
  320.3 1.6 fusion.60
  321.9 8.8 %fusion.61 = f32[896]{0:T(1024)S(1)} fusion(f32[896,4096]{1,0:T(8,128)} %get-tuple-element.233, s32[4096]{0:T(1024)S(1)} %get-tuple-element.264, f32[896]{0:T(1024)S(1)} %max.23, s32[896]{0:T(1024)S(1)} %get-tuple-element.265), kind=kLoop, calls=%fused_computation.6.clone.1 | loop fusion | flops 18349184 | bytes 14707200 | tf_op jit(solution)/shard_map/while/body/eval_jaxpr/reduce_sum | solution.py:61
  331.2 7.7 %fusion.63 = f32[896,128]{1,0:T(8,128)S(1)} fusion(f32[896,4096]{1,0:T(8,128)} %get-tuple-element.233, s32[4096]{0:T(1024)S(1)} %get-tuple-element.264, f32[896]{0:T(1024)S(1)} %add.169, f32[896]{0:T(1024)S(1)} %max.23, s32[896]{0:T(1024)S(1)} %get-tuple-element.265, bf16[2,4096,128]{2,1,0:T(8,128)(2,1)S(1)} %copy-done.7, s32[]{:T(128)S(6)} %copy.72), kind=kOutput, calls=%fused_computation.8.clone.1 | convolution fusion | flops 961544192 | bytes 16216068 | tf_op jit(solution)/shard_map/while/body/eval_jaxpr/dot_general | solution.py:64
  340.8 8.0 %convolution_convert_fusion = bf16[896,5120]{1,0:T(8,128)(2,1)} fusion(bf16[896,256]{0,1:T(8,128)(2,1)} %bitcast.105, bf16[256,5120]{0,1:T(8,128)(2,1)} %all-gather.5.cloned.1.call-done), kind=kOutput, calls=%fused_computation.39 | convolution fusion | flops 2353397760 | bytes 12255232 | tf_op jit(solution)/shard_map/dot_general | solution.py:165
  350.6 1.3 copy.57
  351.9 32.4 %gather_fusion = bf16[4096,2,256]{2,1,0:T(2,128)(2,1)} fusion(bf16[896,2,256]{2,1,0:T(2,128)(2,1)S(1)} %copy.57, s32[4096]{0:T(1024)S(1)} %broadcast_clamp_fusion), kind=kCustom, calls=%fused_computation | custom fusion | bytes 8404992 | tf_op jit(solution)/shard_map/jit(_take)/gather | solution.py:80
  384.3 12.7 %broadcast_select_fusion.1 = bf16[16,256,2,256]{3,2,1,0:T(2,128)(2,1)S(1)} fusion(pred[16,256]{1,0:T(8,128)(4,1)S(1)} %get-tuple-element.172, bf16[16,256,2,256]{3,2,1,0:T(2,128)(2,1)} %bitcast.99, pred[16,256]{1,0:T(8,128)(4,1)S(1)} %get-tuple-element.173), kind=kLoop, calls=%fused_computation.41 | loop fusion | flops 4194304 | bytes 8396800 | tf_op jit(solution)/shard_map/jit(_where)/select_n | solution.py:83
  397.0 109.6 %all_to_all.10 = bf16[16,256,2,256]{3,2,1,0:T(2,128)(2,1)} all-to-all(bf16[16,256,2,256]{3,2,1,0:T(2,128)(2,1)S(1)} %broadcast_select_fusion.1), channel_id=1, replica_groups=mesh['req'=16,'tp'=16] {'req'}, dimensions={0} | all-to-all | bytes 8388608 | tf_op jit(solution)/shard_map/all_to_all | solution.py:88
  506.6 1.3 fusion.34
  507.9 2.1 fusion.37
  510.1 9.2 %copy.79 = bf16[32,128,2,256]{3,2,1,0:T(2,128)(2,1)} copy(bf16[32,128,2,256]{3,2,1,0:T(2,128)(2,1)} %bitcast.100) | data formatting | bytes 8388608
  (100 shorter events, 13.0 us)
Async XLA Ops:
  7.2 143.5 %all-gather.3.cloned.1.call-start = ((), (), s32[]{:S(2)}) async-start(), calls=%async_computation.3 | async-start | bytes 8355840 | tf_op jit(solution)/shard_map/all_gather | solution.py:114
  13.7 11.1 %copy-start.11 = (s32[1,16]{1,0:T(1,128)S(1)}, s32[1,16]{1,0:T(1,128)}, u32[]{:S(2)}) copy-start(s32[1,16]{1,0:T(1,128)} %param.18) | copy-start | bytes 196
  13.7 214.6 %all-to-all-start = ((bf16[16,56,5120]{2,1,0:T(8,128)(2,1)}), bf16[16,56,5120]{2,1,0:T(8,128)(2,1)}, u32[]{:S(2)}, u32[]{:S(2)}) async-start(bf16[16,56,5120]{2,1,0:T(8,128)(2,1)} %stack.10), calls=%async_computation | async-start | bytes 18350080 | tf_op jit(solution)/shard_map/all_to_all | solution.py:107
  24.0 316.8 %all-gather.5.cloned.1.call-start = ((), (), s32[]{:S(2)}) async-start(), calls=%async_computation.4 | async-start | bytes 2785280 | tf_op jit(solution)/shard_map/all_gather | solution.py:163
  24.7 481.9 %reduce-scatter.2.cloned.1.call-start = ((), (), s32[]{:S(2)}) async-start(), calls=%async_computation.5 | async-start | bytes 9748480 | tf_op jit(solution)/shard_map/reduce_scatter | solution.py:164
  46.7 6.6 %copy-start.13 = (s32[1,16]{1,0:T(1,128)S(1)}, s32[1,16]{1,0:T(1,128)}, u32[]{:S(2)}) copy-start(s32[1,16]{1,0:T(1,128)} %param.19) | copy-start | bytes 196
  46.7 6.9 %copy-start.17 = (s32[1,32]{1,0:T(1,128)S(1)}, s32[1,32]{1,0:T(1,128)}, u32[]{:S(2)}) copy-start(s32[1,32]{1,0:T(1,128)} %param.20) | copy-start | bytes 388
  46.7 7.7 %copy-start.15 = (f32[2,256]{1,0:T(2,128)S(1)}, f32[2,256]{1,0:T(2,128)}, u32[]{:S(2)}) copy-start(f32[2,256]{1,0:T(2,128)} %param.15) | copy-start | bytes 6148
  241.5 38.2 %copy-start = (bf16[896,1,256]{0,2,1:T(8,128)(2,1)}, bf16[896,1,256]{0,2,1:T(8,128)(2,1)S(1)}, u32[]{:S(2)}) copy-start(bf16[896,1,256]{0,2,1:T(8,128)(2,1)S(1)} %slice.78) | copy-start | bytes 1376260
  279.7 1.6 copy-start.2
  279.7 1.6 copy-start.4
  292.2 9.3 %copy-start.7 = (bf16[2,4096,128]{2,1,0:T(8,128)(2,1)S(1)}, bf16[2,4096,128]{2,1,0:T(8,128)(2,1)}, u32[]{:S(2)}) copy-start(bf16[2,4096,128]{2,1,0:T(8,128)(2,1)} %get-tuple-element.262) | copy-start | bytes 6291460 | tf_op jit(solution)/shard_map/while
  309.2 1.0 copy-start.8
  310.3 0.8 copy-start.9
  321.9 9.3 %copy-start.7 = (bf16[2,4096,128]{2,1,0:T(8,128)(2,1)S(1)}, bf16[2,4096,128]{2,1,0:T(8,128)(2,1)}, u32[]{:S(2)}) copy-start(bf16[2,4096,128]{2,1,0:T(8,128)(2,1)} %get-tuple-element.262) | copy-start | bytes 6291460 | tf_op jit(solution)/shard_map/while
  338.9 1.0 copy-start.8
  340.0 0.8 copy-start.9
  348.8 0.7 copy-start.12
  348.8 0.7 copy-start.14
  348.8 0.7 copy-start.16
  348.8 1.0 copy-start.3
  348.8 1.2 copy-start.5
  348.8 1.7 copy-start.1
  397.0 111.0 %copy-start.6 = (bf16[56,5120]{1,0:T(8,128)(2,1)S(1)}, bf16[56,5120]{1,0:T(8,128)(2,1)}, u32[]{:S(2)}) copy-start(bf16[56,5120]{1,0:T(8,128)(2,1)} %param.12) | copy-start | bytes 1720324
  397.0 111.0 %copy-start.10 = (f32[5120]{0:T(1024)S(1)}, f32[5120]{0:T(1024)}, u32[]{:S(2)}) copy-start(f32[5120]{0:T(1024)} %param.16) | copy-start | bytes 61444
Sparse Core Ops, SparseCore 0:
  10.8 139.8 all-gather.2
  153.3 77.5 all-gather.4
  349.0 145.7 reduce-scatter.1
